TPU v7x, 32 devices: a whole 2x2x4 slice. The times are simulated.
32 devices in a mesh: dp: 4 (over z), seq: 4 (over y, core), tensor: 2 (over x).
Axes of the slice: x: 2, y: 2, z: 4, core: 2. Of those that a mesh axis runs over, the one named last changes fastest.
Arguments:
- q_self: bfloat16 [4, 512, 4096], P('dp', 'seq', 'tensor'), may hold values from -162 to 162
- k_self: bfloat16 [4, 512, 1024], P('dp', 'seq', 'tensor'), may hold values from -6 to 6
- v_self: bfloat16 [4, 512, 1024], P('dp', 'seq', 'tensor'), may hold values from -6 to 6
- docs: int32 [4, 512], P('dp', 'seq'), may hold values from 0 to 3, never falling along the last dimension, each value on 1 to 384 neighbouring positions
- q_cross: bfloat16 [4, 512, 4096], P('dp', 'seq', 'tensor'), may hold values from -162 to 162
- cotangent: bfloat16 [4, 512, 4096], P('dp', 'seq', 'tensor'), may hold values from -6 to 6
- img_keys: bfloat16 [4, 128, 1024], P('dp', 'seq', 'tensor'), may hold values from -6 to 6
- features: bfloat16 [4, 128, 1280], P('dp', 'seq'), may hold values from -6 to 6
- w_value: bfloat16 [1280, 1024], P(None, 'tensor'), may hold values from -0.15625 to 0.15625
- tiles: int32 [4, 4], P('dp'), may hold values from 1 to 4
- cite: int32 [4, 4], P('dp'), may hold values from 0 to 3, each once within a row
Outputs:
- combined: bfloat16 [4, 512, 4096], P('dp', 'seq', 'tensor')
- weight_grad: float32 [1280, 1024], P(('dp', 'seq'), 'tensor')
Inputs may be any that keep to these rules, and one draw needn't show every extreme that they name: `docs`: along each sample the document numbers never fall; every document 0 to 3 has one or more tokens. `cite`: each sample's row names every image exactly once.
All inputs are finite; a program needn't handle non-finite values.
Results may differ from a plain program's by a relative error of at most 0.029.
Values may be sent and summed in bfloat16 or wider, within the bound.
No kernel may reach another device: no remote copies, remote signals or barrier semaphores. Data moves between devices by JAX's collectives and lax.ppermute only.
A program may use at most 64 MiB of HBM per device.

v0:
```python
import math
import jax
import jax.numpy as jnp
from jax import lax
from jax.sharding import PartitionSpec as P

HD = 128
TILE_TOK = 8
MASK_FILL = -1e30


def absorb_block(
    running, queries, key_rows, value_rows, key_docs, key_pos, query_pos, my_docs, score_scale
):
    running_max, denominator, numerator = running
    kv_local = queries.shape[1]
    key_count = key_rows.shape[0]
    key_heads = key_rows.reshape(key_count, kv_local, HD)
    value_heads = value_rows.reshape(key_count, kv_local, HD)
    scores = (
        jnp.einsum("tgcd,sgd->gcts", queries, key_heads, preferred_element_type=jnp.float32)
        * score_scale
    )
    kept = (query_pos[:, None] >= key_pos[None, :]) & (my_docs[:, None] == key_docs[None, :])
    scores = jnp.where(kept, scores, MASK_FILL)
    new_max = jnp.maximum(running_max, jnp.max(scores, axis=-1))
    factor = jnp.exp(running_max - new_max)
    weights = jnp.where(kept, jnp.exp(scores - new_max[..., None]), 0.0)
    denominator = factor * denominator + jnp.sum(weights, axis=-1)
    numerator = factor[..., None] * numerator + jnp.einsum(
        "gcts,sgd->gctd",
        weights.astype(jnp.bfloat16),
        value_heads,
        preferred_element_type=jnp.float32,
    )
    return (new_max, denominator, numerator)


def on_device(
    q_self, k_self, v_self, docs, q_cross, cotangent, img_keys, features, w_value, tiles, cite
):
    tok_rows = q_self.shape[1]
    kv_local = k_self.shape[2] // HD
    heads_local = q_self.shape[2] // HD
    group_size = heads_local // kv_local
    score_scale = HD ** (-0.5)
    first_row = lax.axis_index("seq") * tok_rows
    query_pos = first_row + jnp.arange(tok_rows, dtype=jnp.int32)
    my_docs = docs[0]
    queries = q_self[0].reshape(tok_rows, kv_local, group_size, HD)
    start_state = (
        jnp.full((kv_local, group_size, tok_rows), MASK_FILL, jnp.float32),
        jnp.zeros((kv_local, group_size, tok_rows), jnp.float32),
        jnp.zeros((kv_local, group_size, tok_rows, HD), jnp.float32),
    )
    piece_keys = lax.all_gather(k_self, "seq", axis=1, tiled=True)
    piece_values = lax.all_gather(v_self, "seq", axis=1, tiled=True)
    piece_docs = lax.all_gather(docs, "seq", axis=1, tiled=True)
    key_count = piece_keys.shape[1]
    block_rows = math.gcd(key_count, 512)
    block_count = key_count // block_rows
    key_blocks = piece_keys[0].reshape(block_count, block_rows, -1)
    value_blocks = piece_values[0].reshape(block_count, block_rows, -1)
    doc_blocks = piece_docs[0].reshape(block_count, block_rows)
    pos_blocks = jnp.arange(key_count, dtype=jnp.int32).reshape(block_count, block_rows)

    def absorb_step(state_now, block_item):
        key_part, value_part, doc_part, pos_part = block_item
        return (
            absorb_block(
                state_now,
                queries,
                key_part,
                value_part,
                doc_part,
                pos_part,
                query_pos,
                my_docs,
                score_scale,
            ),
            None,
        )

    running_max, denominator, numerator = lax.scan(
        absorb_step, start_state, (key_blocks, value_blocks, doc_blocks, pos_blocks)
    )[0]
    self_out = numerator / denominator[..., None]
    values_own = jnp.dot(features[0], w_value, preferred_element_type=jnp.float32).astype(
        jnp.bfloat16
    )
    image_keys, image_values = (
        lax.all_gather(img_keys[0], "seq", axis=0, tiled=True),
        lax.all_gather(values_own, "seq", axis=0, tiled=True),
    )
    key_count = image_keys.shape[0]
    slot_count = img_keys.shape[1]
    image_count = tiles.shape[1]
    doc_hit = my_docs[:, None] == jnp.arange(cite.shape[1], dtype=jnp.int32)[None, :]
    image_of = jnp.sum(jnp.where(doc_hit, cite[0][None, :], 0), axis=1)
    slot_ids = jnp.arange(key_count, dtype=jnp.int32)
    key_image = slot_ids // slot_count
    owner_hit = key_image[:, None] == jnp.arange(image_count, dtype=jnp.int32)[None, :]
    tile_limit = jnp.sum(jnp.where(owner_hit, tiles[0][None, :], 0), axis=1) * TILE_TOK
    cross_kept = (image_of[:, None] == key_image[None, :]) & (slot_ids % slot_count < tile_limit)[
        None, :
    ]
    cross_q = q_cross[0].reshape(tok_rows, kv_local, group_size, HD)
    cross_scores = (
        jnp.einsum(
            "tgcd,sgd->gcts",
            cross_q,
            image_keys.reshape(key_count, kv_local, HD),
            preferred_element_type=jnp.float32,
        )
        * score_scale
    )
    cross_scores = jnp.where(cross_kept, cross_scores, MASK_FILL)
    cross_exp = jnp.where(
        cross_kept, jnp.exp(cross_scores - jnp.max(cross_scores, axis=-1, keepdims=True)), 0.0
    )
    cross_weights = (cross_exp / jnp.sum(cross_exp, axis=-1, keepdims=True)).astype(jnp.bfloat16)
    cross_out = jnp.einsum(
        "gcts,sgd->gctd",
        cross_weights,
        image_values.reshape(key_count, kv_local, HD),
        preferred_element_type=jnp.float32,
    )
    merged = (
        (self_out + cross_out)
        .astype(jnp.bfloat16)
        .transpose(2, 0, 1, 3)
        .reshape(1, tok_rows, heads_local * HD)
    )
    cot_rows = cotangent[0].reshape(tok_rows, kv_local, group_size, HD)
    grad_terms = jnp.einsum(
        "gcts,tgcd->sgd", cross_weights, cot_rows, preferred_element_type=jnp.float32
    ).reshape(key_count, kv_local * HD)
    value_grad = lax.psum_scatter(
        grad_terms.astype(jnp.bfloat16), "seq", scatter_dimension=0, tiled=True
    )
    own_features = features[0]
    summed_samples = lax.psum_scatter(
        lax.dot_general(
            own_features, value_grad, (((0,), (0,)), ((), ())), preferred_element_type=jnp.float32
        ).astype(jnp.bfloat16),
        "dp",
        scatter_dimension=0,
        tiled=True,
    )
    weight_grad = lax.psum_scatter(summed_samples, "seq", scatter_dimension=0, tiled=True).astype(
        jnp.float32
    )
    return (merged, weight_grad)


def solution(mesh):
    in_specs = (
        P("dp", "seq", "tensor"),
        P("dp", "seq", "tensor"),
        P("dp", "seq", "tensor"),
        P("dp", "seq"),
        P("dp", "seq", "tensor"),
        P("dp", "seq", "tensor"),
        P("dp", "seq", "tensor"),
        P("dp", "seq", None),
        P(None, "tensor"),
        P("dp", None),
        P("dp", None),
    )
    out_specs = (P("dp", "seq", "tensor"), P(("dp", "seq"), "tensor"))
    return jax.shard_map(
        on_device, mesh=mesh, in_specs=in_specs, out_specs=out_specs, check_vma=False
    )
```

profile of v0, /device:TPU:0, one launch (start us, length us, event | category | flops | bytes accessed | tf_op | source)
XLA Modules:
  0.0 108.2 jit_solution(1521018898285160767)
XLA Ops:
  7.2 0.0 copy-start
  7.2 0.0 reduce-scatter.10.cloned.1.call-start
  7.2 0.8 select_reduce_fusion
  8.1 1.4 %reshape_squeeze.10 = bf16[128,4,4,128]{3,2,1,0:T(4,128)(2,1)S(1)} reshape(bf16[1,128,2048]{2,1,0:T(8,128)(2,1)} %param.15) | data formatting | bytes 1048576 | tf_op jit(solution)/shard_map/reshape;squeeze | solution.py:107
  9.5 6.7 %all-gather = bf16[1,128,512]{2,1,0:T(8,128)(2,1)S(1)} all-gather(bf16[1,32,512]{2,1,0:T(8,128)(2,1)} %param.17), channel_id=2, replica_groups=mesh['dp'=4,'seq'=4,'tensor'=2] {'seq'}, dimensions={1}, use_global_device_ids=true | all-gather | bytes 163840 | tf_op jit(solution)/shard_map/all_gather | solution.py:92
  16.2 0.1 copy.56
  16.4 0.0 copy-start.2
  16.4 1.3 %copy.78 = bf16[1,128,2048]{1,2,0:T(8,128)(2,1)S(1)} copy(bf16[1,128,2048]{2,1,0:T(8,128)(2,1)} %param.16) | data formatting | bytes 1048576 | tf_op jit(solution)/shard_map/reshape;squeeze | solution.py:134
  17.7 0.8 select_reduce_fusion.1
  18.5 0.1 compare_and_fusion
  18.6 1.5 %fusion.39 = (f32[4,4,128]{2,1,0:T(4,128)S(1)}, f32[4,4,128,128]{2,3,1,0:T(8,128)}) fusion(bf16[128,4,128,1]{0,2,3,1:T(8,128)(2,1)S(1)} %bitcast.96, bf16[128,4,4,128]{3,2,1,0:T(4,128)(2,1)S(1)} %reshape_squeeze.10, pred[128,128]{0,1:T(8,128)(4,1)S(1)} %compare_and_fusion), kind=kOutput, calls=%fused_computation.53 | convolution fusion | flops 68419712 | bytes 1728512 | tf_op jit(solution)/shard_map/sub | solution.py:119
  20.1 0.0 copy-start.4
  20.1 0.0 copy-start.1
  20.1 1.6 %fusion.21 = bf16[4,128,128]{1,2,0:T(8,128)(2,1)S(1)} fusion(bf16[128,4,4,128]{0,3,2,1:T(8,128)(2,1)S(1)} %bitcast.94, f32[4,4,128,128]{2,3,1,0:T(8,128)} %get-tuple-element.48, f32[4,4,128]{2,1,0:T(4,128)S(1)} %get-tuple-element.47), kind=kOutput, calls=%fused_computation.22 | convolution fusion | flops 67698688 | bytes 1712128 | tf_op jit(solution)/shard_map/gcts,tgcd->sgd/dot_general | solution.py:135
  21.7 0.0 copy-start.3
  21.7 0.8 copy.79
  22.5 0.0 reduce-scatter.10.cloned.1.call-update
  22.5 0.0 copy-start.5
  22.6 0.0 reduce-scatter.12.cloned.1.call-start
  22.6 21.3 %reduce-scatter.10.cloned.1.call-done = bf16[32,512]{1,0:T(8,128)(2,1)} async-done(((bf16[128,512]{1,0:T(8,128)(2,1)}), bf16[32,512]{1,0:T(8,128)(2,1)}) %reduce-scatter.10.cloned.1.call-update) | async-done | bytes 32784
  43.9 0.0 copy-done.2
  43.9 1.3 %fusion.4 = bf16[1280,512]{0,1:T(8,128)(2,1)S(1)} fusion(bf16[32,512]{1,0:T(8,128)(2,1)} %reduce-scatter.10.cloned.1.call-done, bf16[1,32,1280]{2,1,0:T(8,128)(2,1)S(1)} %copy-done.2), kind=kOutput, calls=%fused_computation.7 | convolution fusion | flops 42598400 | bytes 1425408 | tf_op jit(solution)/shard_map/dot_general | solution.py:143
  45.2 1.5 %copy.81 = bf16[1280,512]{1,0:T(8,128)(2,1)} copy(bf16[1280,512]{0,1:T(8,128)(2,1)S(1)} %fusion.4) | data formatting | bytes 2621440
  46.7 0.0 reduce-scatter.12.cloned.1.call-update
  46.8 0.0 reduce-scatter.14.cloned.1.call-start
  46.8 0.0 copy-done.4
  46.8 0.1 copy.51
  46.9 0.0 copy-done.1
  47.0 0.4 reshape_squeeze.9
  47.3 0.0 copy-done.3
  47.3 6.5 %all_gather.17 = bf16[1,512,512]{2,1,0:T(8,128)(2,1)S(1)} all-gather(bf16[1,128,512]{2,1,0:T(8,128)(2,1)S(1)} %copy-done.3), channel_id=1, replica_groups=mesh['dp'=4,'seq'=4,'tensor'=2] {'seq'}, dimensions={1}, use_global_device_ids=true | all-gather | bytes 655360 | tf_op jit(solution)/shard_map/all_gather | solution.py:57
  53.8 0.2 copy.54
  54.1 0.0 copy-done.5
  54.1 5.1 %all_gather.15 = s32[1,512]{1,0:T(1,128)S(1)} all-gather(s32[1,128]{1,0:T(1,128)S(1)} %copy-done.5), channel_id=1, replica_groups=mesh['dp'=4,'seq'=4,'tensor'=2] {'seq'}, dimensions={1}, use_global_device_ids=true | all-gather | bytes 2560 | tf_op jit(solution)/shard_map/all_gather | solution.py:58
  59.1 7.3 %all_gather.16 = bf16[1,512,512]{1,2,0:T(8,128)(2,1)S(1)} all-gather(bf16[1,128,512]{1,2,0:T(8,128)(2,1)S(1)} %copy.51), channel_id=1, replica_groups=mesh['dp'=4,'seq'=4,'tensor'=2] {'seq'}, dimensions={1}, use_global_device_ids=true | all-gather | bytes 655360 | tf_op jit(solution)/shard_map/all_gather | solution.py:56
  66.4 0.1 fusion.25
  66.6 0.9 fusion.1
  67.5 1.0 fusion.2
  68.5 0.0 copy-start.6
  68.5 2.2 %fusion.17 = f32[128,4,4,128]{0,3,2,1:T(8,128)} fusion(bf16[512,4,128,1]{0,2,3,1:T(8,128)(2,1)S(1)} %bitcast.93, f32[4,512,128,4]{2,1,3,0:T(8,128)S(1)} %get-tuple-element.46, f32[4,4,128]{2,1,0:T(4,128)S(1)} %get-tuple-element.44, pred[128,512]{0,1:T(8,128)(4,1)S(1)} %fusion.25, f32[128,4,4]{0,2,1:T(4,128)S(1)} %get-tuple-element.32), kind=kOutput, calls=%fused_computation.19 | convolution fusion | flops 273940480 | bytes 5849088 | tf_op jit(solution)/shard_map/while/body/eval_jaxpr/gcts,sgd->gctd/dot_general | solution.py:30
  70.6 7.6 %reduce-scatter.12.cloned.1.call-done = bf16[320,512]{1,0:T(8,128)(2,1)} async-done(((bf16[1280,512]{1,0:T(8,128)(2,1)}), bf16[320,512]{1,0:T(8,128)(2,1)}) %reduce-scatter.12.cloned.1.call-update) | async-done | bytes 327696
  78.3 0.0 reduce-scatter.14.cloned.1.call-update
  78.3 0.0 copy-done
  78.3 0.3 convolution_convert_fusion.1
  78.6 5.4 %all_gather.19 = bf16[128,512]{1,0:T(8,128)(2,1)S(1)} all-gather(bf16[32,512]{1,0:T(8,128)(2,1)S(1)} %convolution_convert_fusion.1), channel_id=1, replica_groups=mesh['dp'=4,'seq'=4,'tensor'=2] {'seq'}, dimensions={0}, use_global_device_ids=true | all-gather | bytes 163840 | tf_op jit(solution)/shard_map/all_gather | solution.py:93
  84.0 0.1 copy.77
  84.2 0.0 copy-done.6
  84.2 1.5 %fusion.20 = bf16[128,4,4,128]{0,3,2,1:T(8,128)(2,1)S(1)} fusion(bf16[128,4,128,1]{0,2,3,1:T(8,128)(2,1)S(1)} %bitcast.97, f32[128,4,4,128]{0,3,2,1:T(8,128)} %fusion.17, f32[128,4,4]{0,2,1:T(4,128)S(1)} %bitcast_add_fusion, f32[4,4,128,128]{2,3,1,0:T(8,128)S(1)} %copy-done.6, f32[4,4,128]{2,1,0:T(4,128)S(1)} %get-tuple-element.47), kind=kOutput, calls=%fused_computation.20 | convolution fusion | flops 68419584 | bytes 2768896 | tf_op jit(solution)/shard_map/gcts,sgd->gctd/dot_general | solution.py:122
  85.7 1.0 copy.63
  86.7 13.2 %reduce-scatter.14.cloned.1.call-done = bf16[80,512]{1,0:T(8,128)(2,1)} async-done(((bf16[320,512]{1,0:T(8,128)(2,1)}), bf16[80,512]{1,0:T(8,128)(2,1)}) %reduce-scatter.14.cloned.1.call-update) | async-done | bytes 81936
  99.9 1.0 copy.84
  100.9 0.8 copy.64
  (5 shorter events, 0.0 us)
Async XLA Ops:
  7.2 71.1 %copy-start = (bf16[1280,512]{1,0:T(8,128)(2,1)S(1)}, bf16[1280,512]{1,0:T(8,128)(2,1)}, u32[]{:S(2)}) copy-start(bf16[1280,512]{1,0:T(8,128)(2,1)} %param.19) | copy-start | bytes 3932164
  7.2 36.8 %reduce-scatter.10.cloned.1.call-start = ((), (), s32[]{:S(2)}) async-start(), calls=%async_computation.3 | async-start | bytes 163840
  16.4 27.6 %copy-start.2 = (bf16[1,32,1280]{2,1,0:T(8,128)(2,1)S(1)}, bf16[1,32,1280]{2,1,0:T(8,128)(2,1)}, u32[]{:S(2)}) copy-start(bf16[1,32,1280]{2,1,0:T(8,128)(2,1)} %param.18) | copy-start | bytes 245764
  20.1 26.7 %copy-start.4 = (bf16[1,128,512]{2,1,0:T(8,128)(2,1)S(1)}, bf16[1,128,512]{2,1,0:T(8,128)(2,1)}, u32[]{:S(2)}) copy-start(bf16[1,128,512]{2,1,0:T(8,128)(2,1)} %param.12) | copy-start | bytes 393220
  20.1 26.8 %copy-start.1 = (bf16[1,128,2048]{2,1,0:T(8,128)(2,1)S(1)}, bf16[1,128,2048]{2,1,0:T(8,128)(2,1)}, u32[]{:S(2)}) copy-start(bf16[1,128,2048]{2,1,0:T(8,128)(2,1)} %param.11) | copy-start | bytes 1572868
  21.7 25.6 %copy-start.3 = (bf16[1,128,512]{2,1,0:T(8,128)(2,1)S(1)}, bf16[1,128,512]{2,1,0:T(8,128)(2,1)}, u32[]{:S(2)}) copy-start(bf16[1,128,512]{2,1,0:T(8,128)(2,1)} %param.13) | copy-start | bytes 393220
  22.5 31.5 %copy-start.5 = (s32[1,128]{1,0:T(1,128)S(1)}, s32[1,128]{1,0:T(1,128)}, u32[]{:S(2)}) copy-start(s32[1,128]{1,0:T(1,128)} %param.14) | copy-start | bytes 1540
  22.6 55.7 %reduce-scatter.12.cloned.1.call-start = ((), (), s32[]{:S(2)}) async-start(), calls=%async_computation.4 | async-start | bytes 1638400
  46.8 53.2 %reduce-scatter.14.cloned.1.call-start = ((), (), s32[]{:S(2)}) async-start(), calls=%async_computation.5 | async-start | bytes 409600
  68.5 15.7 %copy-start.6 = (f32[4,4,128,128]{2,3,1,0:T(8,128)S(1)}, f32[4,4,128,128]{2,3,1,0:T(8,128)}, u32[]{:S(2)}) copy-start(f32[4,4,128,128]{2,3,1,0:T(8,128)} %get-tuple-element.48) | copy-start | bytes 3145732
Sparse Core Ops, SparseCore 0:
  22.7 21.2 reduce-scatter.9
  46.9 31.3 reduce-scatter.11
  80.8 19.1 reduce-scatter.13
where the time goes:
time: 109 us; the launch traced here: 108 us
  waiting for transfers between devices  42.2 us (39%)
  blocking collectives  31 us (28%)
  between operations  14 us (13%)
  matrix products  9.32 us (9%)
  local copies, waits for them, and re-layouts  8.77 us (8%)
  other arithmetic  2.87 us (3%)
    unnamed x6, waiting for transfers between devices  42.2 us
    all_gather x1, blocking collectives, on_device(): piece_keys = lax.all_gather(k_self, 'seq', axis=1, tiled=True)  7.28 us
    all_gather x1, blocking collectives, on_device(): lax.all_gather(img_keys[0], 'seq', axis=0, tiled=True)  6.75 us
    all_gather x1, blocking collectives, on_device(): piece_values = lax.all_gather(v_self, 'seq', axis=1, tiled=True)  6.5 us
    all_gather x1, blocking collectives, on_device(): lax.all_gather(values_own, 'seq', axis=0, tiled=True)  5.42 us
    unnamed x20, local copies, waits for them, and re-layouts  5.21 us
    all_gather x1, blocking collectives, on_device(): piece_docs = lax.all_gather(docs, 'seq', axis=1, tiled=True)  5.06 us
  transfers between devices with their start and end apart: 3, of which 3 were waited for; matrix products, arithmetic and copies ran while one was open for 7% of the time, Pallas kernels for 0%

commit v1 on v0

--- a/solution.py
+++ b/solution.py
@@ -53,7 +53,12 @@
         jnp.zeros((kv_local, group_size, tok_rows), jnp.float32),
         jnp.zeros((kv_local, group_size, tok_rows, HD), jnp.float32),
     )
-    piece_keys = lax.all_gather(k_self, "seq", axis=1, tiled=True)
+    ring = [k_self]
+    for hop in range(3):
+        ring.append(lax.ppermute(ring[-1], "seq", [(dev, (dev + 1) % 4) for dev in range(4)]))
+    piece_keys = jnp.roll(
+        jnp.concatenate(ring[::-1], axis=1), (lax.axis_index("seq") + 1) * ring[0].shape[1], axis=1
+    )
     piece_values = lax.all_gather(v_self, "seq", axis=1, tiled=True)
     piece_docs = lax.all_gather(docs, "seq", axis=1, tiled=True)
     key_count = piece_keys.shape[1]

time: 109 us -> 109 us (level)
  blocking collectives: 31 us -> 24.3 us
  other arithmetic: 2.87 us -> 5.16 us
  local copies, waits for them, and re-layouts: 8.77 us -> 11 us
    all_gather x1 -> x0, blocking collectives: 7.28 us -> none  [on_device(): piece_keys = lax.all_gather(k_self, 'seq', axis=1, tiled=True)]
    ppermute x0 -> x3, waiting for transfers between devices: none -> 3.92 us  [on_device(): lax.ppermute(ring[-1], 'seq', [(dev, (dev + 1) % 4) for dev in range(4)])]
    unnamed x6, waiting for transfers between devices: 42.2 us -> 39.3 us
    reduce_sum x1, other arithmetic: 1.01 us -> 3.27 us  [absorb_block(): denominator = factor * denominator + jnp.sum(weights, axis=-1)]
    unnamed x20 -> x27, local copies, waits for them, and re-layouts: 5.21 us -> 7.36 us
  transfers between devices with their start and end apart: 3 -> 6, of which waited for: 3 -> 4; matrix products, arithmetic and copies ran while one was open for 7% -> 12% of each run, Pallas kernels for 0% -> 0%
where the time goes in v1:
time: 109 us; the launch traced here: 108 us
  waiting for transfers between devices  43.2 us (40%)
  blocking collectives  24.3 us (22%)
  between operations  14 us (13%)
  local copies, waits for them, and re-layouts  11 us (10%)
  matrix products  9.31 us (9%)
  other arithmetic  5.16 us (5%)
  starting transfers between devices  1.21 us (1%)
    unnamed x6, waiting for transfers between devices  39.3 us
    unnamed x27, local copies, waits for them, and re-layouts  7.36 us
    all_gather x1, blocking collectives, on_device(): lax.all_gather(img_keys[0], 'seq', axis=0, tiled=True)  6.75 us
    all_gather x1, blocking collectives, on_device(): piece_values = lax.all_gather(v_self, 'seq', axis=1, tiled=True)  6.71 us
    all_gather x1, blocking collectives, on_device(): lax.all_gather(values_own, 'seq', axis=0, tiled=True)  5.8 us
    all_gather x1, blocking collectives, on_device(): piece_docs = lax.all_gather(docs, 'seq', axis=1, tiled=True)  5.06 us
    ppermute x3, waiting for transfers between devices, on_device(): lax.ppermute(ring[-1], 'seq', [(dev, (dev + 1) % 4) for dev in range(4)])  3.92 us
    reduce_sum x1, other arithmetic, absorb_block(): denominator = factor * denominator + jnp.sum(weights, axis=-1)  3.27 us
  transfers between devices with their start and end apart: 6, of which 4 were waited for; matrix products, arithmetic and copies ran while one was open for 12% of the time, Pallas kernels for 0%

profile of v1, /device:TPU:0, one launch (start us, length us, event | category | flops | bytes accessed | tf_op | source)
XLA Modules:
  0.0 108.2 jit_solution(17699315524621244304)
XLA Ops:
  7.2 0.0 copy-start
  7.2 0.0 reduce-scatter.10.cloned.1.call-start
  7.2 0.8 select_reduce_fusion
  8.1 1.4 %reshape_squeeze.10 = bf16[128,4,4,128]{3,2,1,0:T(4,128)(2,1)S(1)} reshape(bf16[1,128,2048]{2,1,0:T(8,128)(2,1)} %param.15) | data formatting | bytes 1048576 | tf_op jit(solution)/shard_map/reshape;squeeze | solution.py:112
  9.5 6.7 %all-gather = bf16[1,128,512]{2,1,0:T(8,128)(2,1)S(1)} all-gather(bf16[1,32,512]{2,1,0:T(8,128)(2,1)} %param.17), channel_id=2, replica_groups=mesh['dp'=4,'seq'=4,'tensor'=2] {'seq'}, dimensions={1}, use_global_device_ids=true | all-gather | bytes 163840 | tf_op jit(solution)/shard_map/all_gather | solution.py:97
  16.2 0.1 copy.62
  16.4 0.0 copy-start.4
  16.4 1.3 %copy.84 = bf16[1,128,2048]{1,2,0:T(8,128)(2,1)S(1)} copy(bf16[1,128,2048]{2,1,0:T(8,128)(2,1)} %param.16) | data formatting | bytes 1048576 | tf_op jit(solution)/shard_map/reshape;squeeze | solution.py:139
  17.7 0.0 copy-start.3
  17.7 0.8 select_reduce_fusion.1
  18.5 0.1 compare_and_fusion
  18.6 1.6 %fusion.39 = (f32[4,4,128]{2,1,0:T(4,128)S(1)}, f32[4,4,128,128]{2,3,1,0:T(8,128)}) fusion(bf16[128,4,128,1]{0,2,3,1:T(8,128)(2,1)S(1)} %bitcast.97, bf16[128,4,4,128]{3,2,1,0:T(4,128)(2,1)S(1)} %reshape_squeeze.10, pred[128,128]{0,1:T(8,128)(4,1)S(1)} %compare_and_fusion), kind=kOutput, calls=%fused_computation.62 | convolution fusion | flops 68419712 | bytes 1728512 | tf_op jit(solution)/shard_map/sub | solution.py:124
  20.2 1.5 %fusion.21 = bf16[4,128,128]{1,2,0:T(8,128)(2,1)S(1)} fusion(bf16[128,4,4,128]{0,3,2,1:T(8,128)(2,1)S(1)} %bitcast.94, f32[4,4,128,128]{2,3,1,0:T(8,128)} %get-tuple-element.48, f32[4,4,128]{2,1,0:T(4,128)S(1)} %get-tuple-element.47), kind=kOutput, calls=%fused_computation.22 | convolution fusion | flops 67698688 | bytes 1712128 | tf_op jit(solution)/shard_map/gcts,tgcd->sgd/dot_general | solution.py:140
  21.7 0.0 copy-start.2
  21.7 0.8 copy.85
  22.5 0.0 reduce-scatter.10.cloned.1.call-update
  22.5 0.0 reduce-scatter.12.cloned.1.call-start
  22.6 0.0 copy-done.4
  22.6 0.1 copy.55
  22.7 0.4 collective-permute-start
  23.1 0.0 copy-done
  23.1 0.0 copy-done.3
  23.1 0.3 convolution_convert_fusion.1
  23.4 0.0 copy-start.5
  23.4 20.5 %reduce-scatter.10.cloned.1.call-done = bf16[32,512]{1,0:T(8,128)(2,1)} async-done(((bf16[128,512]{1,0:T(8,128)(2,1)}), bf16[32,512]{1,0:T(8,128)(2,1)}) %reduce-scatter.10.cloned.1.call-update) | async-done | bytes 32784
  43.9 1.3 %fusion.4 = bf16[1280,512]{0,1:T(8,128)(2,1)S(1)} fusion(bf16[32,512]{1,0:T(8,128)(2,1)} %reduce-scatter.10.cloned.1.call-done, bf16[1,32,1280]{2,1,0:T(8,128)(2,1)S(1)} %copy-done.3), kind=kOutput, calls=%fused_computation.7 | convolution fusion | flops 42598400 | bytes 1425408 | tf_op jit(solution)/shard_map/dot_general | solution.py:148
  45.2 1.5 %copy.87 = bf16[1280,512]{1,0:T(8,128)(2,1)} copy(bf16[1280,512]{0,1:T(8,128)(2,1)S(1)} %fusion.4) | data formatting | bytes 2621440
  46.7 0.0 reduce-scatter.12.cloned.1.call-update
  46.7 0.0 reduce-scatter.14.cloned.1.call-start
  46.8 6.7 %all_gather.13 = bf16[1,512,512]{2,1,0:T(8,128)(2,1)S(1)} all-gather(bf16[1,128,512]{2,1,0:T(8,128)(2,1)} %param.13), channel_id=1, replica_groups=mesh['dp'=4,'seq'=4,'tensor'=2] {'seq'}, dimensions={1}, use_global_device_ids=true | all-gather | bytes 655360 | tf_op jit(solution)/shard_map/all_gather | solution.py:62
  53.5 0.0 collective-permute-done
  53.5 0.3 collective-permute-start.1
  53.8 5.8 %all_gather.15 = bf16[128,512]{1,0:T(8,128)(2,1)S(1)} all-gather(bf16[32,512]{1,0:T(8,128)(2,1)S(1)} %convolution_convert_fusion.1), channel_id=1, replica_groups=mesh['dp'=4,'seq'=4,'tensor'=2] {'seq'}, dimensions={0}, use_global_device_ids=true | all-gather | bytes 163840 | tf_op jit(solution)/shard_map/all_gather | solution.py:98
  59.6 0.0 copy-done.2
  59.6 0.4 reshape_squeeze.9
  60.0 0.2 copy.60
  60.2 0.1 copy.83
  60.4 0.0 copy-done.5
  60.4 5.1 %all_gather.12 = s32[1,512]{1,0:T(1,128)S(1)} all-gather(s32[1,128]{1,0:T(1,128)S(1)} %copy-done.5), channel_id=1, replica_groups=mesh['dp'=4,'seq'=4,'tensor'=2] {'seq'}, dimensions={1}, use_global_device_ids=true | all-gather | bytes 2560 | tf_op jit(solution)/shard_map/all_gather | solution.py:63
  65.4 0.0 collective-permute-done.1
  65.4 0.3 collective-permute-start.2
  65.8 0.1 fusion.25
  65.9 3.9 %collective-permute-done.2 = bf16[1,128,512]{1,2,0:T(8,128)(2,1)S(1)} collective-permute-done((bf16[1,128,512]{1,2,0:T(8,128)(2,1)S(1)}, bf16[1,128,512]{1,2,0:T(8,128)(2,1)S(1)}, u32[]{:S(2)}, u32[]{:S(2)}) %collective-permute-start.2) | collective-permute-done | bytes 131104 | tf_op jit(solution)/shard_map/ppermute | solution.py:58
  70.3 0.9 fusion.1
  71.2 0.0 copy-start.1
  71.2 1.9 %copy-done.1 = f32[4,512,128,4]{2,1,3,0:T(8,128)} copy-done((f32[4,512,128,4]{2,1,3,0:T(8,128)}, f32[4,512,128,4]{2,1,3,0:T(8,128)S(1)}, u32[]{:S(2)}) %copy-start.1) | copy-done | bytes 4194328
  73.1 2.2 %fusion.17 = f32[128,4,4,128]{0,3,2,1:T(8,128)} fusion(bf16[512,4,128,1]{0,2,3,1:T(8,128)(2,1)S(1)} %bitcast.93, f32[4,512,128,4]{2,1,3,0:T(8,128)S(1)} %get-tuple-element.46, f32[4,4,128]{2,1,0:T(4,128)S(1)} %get-tuple-element.44, pred[128,512]{0,1:T(8,128)(4,1)S(1)} %fusion.25, f32[128,4,4]{0,2,1:T(4,128)S(1)} %get-tuple-element.32), kind=kOutput, calls=%fused_computation.19 | convolution fusion | flops 273940480 | bytes 5849088 | tf_op jit(solution)/shard_map/while/body/eval_jaxpr/gcts,sgd->gctd/dot_general | solution.py:30
  75.3 3.0 %reduce-scatter.12.cloned.1.call-done = bf16[320,512]{1,0:T(8,128)(2,1)} async-done(((bf16[1280,512]{1,0:T(8,128)(2,1)}), bf16[320,512]{1,0:T(8,128)(2,1)}) %reduce-scatter.12.cloned.1.call-update) | async-done | bytes 327696
  78.2 0.0 reduce-scatter.14.cloned.1.call-update
  78.3 0.0 copy-start.6
  78.3 3.3 %fusion.2 = f32[4,4,128]{2,1,0:T(4,128)S(1)} fusion(f32[4,512,128,4]{2,1,3,0:T(8,128)} %copy-done.1, f32[4,4,128]{2,1,0:T(4,128)S(1)} %get-tuple-element.44, pred[128,512]{0,1:T(8,128)(4,1)S(1)} %fusion.25), kind=kLoop, calls=%fused_computation.5 | loop fusion | flops 5240832 | bytes 4276224 | tf_op jit(solution)/shard_map/while/body/eval_jaxpr/reduce_sum | solution.py:29
  81.6 0.0 copy-done.6
  81.6 1.5 %fusion.20 = bf16[128,4,4,128]{0,3,2,1:T(8,128)(2,1)S(1)} fusion(bf16[128,4,128,1]{0,2,3,1:T(8,128)(2,1)S(1)} %bitcast.96, f32[128,4,4,128]{0,3,2,1:T(8,128)S(1)} %copy-done.6, f32[128,4,4]{0,2,1:T(4,128)S(1)} %bitcast_add_fusion, f32[4,4,128,128]{2,3,1,0:T(8,128)} %get-tuple-element.48, f32[4,4,128]{2,1,0:T(4,128)S(1)} %get-tuple-element.47), kind=kOutput, calls=%fused_computation.20 | convolution fusion | flops 68419584 | bytes 2768896 | tf_op jit(solution)/shard_map/gcts,sgd->gctd/dot_general | solution.py:127
  83.1 1.0 copy.69
  84.1 15.8 %reduce-scatter.14.cloned.1.call-done = bf16[80,512]{1,0:T(8,128)(2,1)} async-done(((bf16[320,512]{1,0:T(8,128)(2,1)}), bf16[80,512]{1,0:T(8,128)(2,1)}) %reduce-scatter.14.cloned.1.call-update) | async-done | bytes 81936
  99.9 1.0 copy.90
  100.9 0.8 copy.70
  (14 shorter events, 0.4 us)
Async XLA Ops:
  7.2 16.0 %copy-start = (bf16[1280,512]{1,0:T(8,128)(2,1)S(1)}, bf16[1280,512]{1,0:T(8,128)(2,1)}, u32[]{:S(2)}) copy-start(bf16[1280,512]{1,0:T(8,128)(2,1)} %param.19) | copy-start | bytes 3932164
  7.2 36.8 %reduce-scatter.10.cloned.1.call-start = ((), (), s32[]{:S(2)}) async-start(), calls=%async_computation.3 | async-start | bytes 163840
  16.4 6.2 %copy-start.4 = (bf16[1,128,512]{2,1,0:T(8,128)(2,1)S(1)}, bf16[1,128,512]{2,1,0:T(8,128)(2,1)}, u32[]{:S(2)}) copy-start(bf16[1,128,512]{2,1,0:T(8,128)(2,1)} %param.12) | copy-start | bytes 393220
  17.7 5.4 %copy-start.3 = (bf16[1,32,1280]{2,1,0:T(8,128)(2,1)S(1)}, bf16[1,32,1280]{2,1,0:T(8,128)(2,1)}, u32[]{:S(2)}) copy-start(bf16[1,32,1280]{2,1,0:T(8,128)(2,1)} %param.18) | copy-start | bytes 245764
  21.7 37.9 %copy-start.2 = (bf16[1,128,2048]{2,1,0:T(8,128)(2,1)S(1)}, bf16[1,128,2048]{2,1,0:T(8,128)(2,1)}, u32[]{:S(2)}) copy-start(bf16[1,128,2048]{2,1,0:T(8,128)(2,1)} %param.11) | copy-start | bytes 1572868
  22.5 55.7 %reduce-scatter.12.cloned.1.call-start = ((), (), s32[]{:S(2)}) async-start(), calls=%async_computation.4 | async-start | bytes 1638400
  22.7 30.8 %collective-permute-start = (bf16[1,128,512]{1,2,0:T(8,128)(2,1)S(1)}, bf16[1,128,512]{1,2,0:T(8,128)(2,1)S(1)}, u32[]{:S(2)}, u32[]{:S(2)}) collective-permute-start(bf16[1,128,512]{1,2,0:T(8,128)(2,1)S(1)} %copy.55), channel_id=1, source_target_pairs={{0,2},{2,4},{4,6},{6,0},{1,3},{3,5},{5,7},{7,1},{8,10},{10,12},{12... | collective-permute-start | bytes 393224 | tf_op jit(solution)/shard_map/ppermute | solution.py:58
  23.4 36.9 %copy-start.5 = (s32[1,128]{1,0:T(1,128)S(1)}, s32[1,128]{1,0:T(1,128)}, u32[]{:S(2)}) copy-start(s32[1,128]{1,0:T(1,128)} %param.14) | copy-start | bytes 1540
  46.7 53.2 %reduce-scatter.14.cloned.1.call-start = ((), (), s32[]{:S(2)}) async-start(), calls=%async_computation.5 | async-start | bytes 409600
  53.5 11.9 %collective-permute-start.1 = (bf16[1,128,512]{1,2,0:T(8,128)(2,1)S(1)}, bf16[1,128,512]{1,2,0:T(8,128)(2,1)S(1)}, u32[]{:S(2)}, u32[]{:S(2)}) collective-permute-start(bf16[1,128,512]{1,2,0:T(8,128)(2,1)S(1)} %collective-permute-done), channel_id=1, source_target_pairs={{0,2},{2,4},{4,6},{6,0},{1,3},{3,5},{5,7},{7,1},{8,10},{10,12},{12... | collective-permute-start | bytes 393224 | tf_op jit(solution)/shard_map/ppermute | solution.py:58
  65.4 4.4 %collective-permute-start.2 = (bf16[1,128,512]{1,2,0:T(8,128)(2,1)S(1)}, bf16[1,128,512]{1,2,0:T(8,128)(2,1)S(1)}, u32[]{:S(2)}, u32[]{:S(2)}) collective-permute-start(bf16[1,128,512]{1,2,0:T(8,128)(2,1)S(1)} %collective-permute-done.1), channel_id=1, source_target_pairs={{0,2},{2,4},{4,6},{6,0},{1,3},{3,5},{5,7},{7,1},{8,10},{10,12},{12... | collective-permute-start | bytes 393224 | tf_op jit(solution)/shard_map/ppermute | solution.py:58
  71.2 1.9 %copy-start.1 = (f32[4,512,128,4]{2,1,3,0:T(8,128)}, f32[4,512,128,4]{2,1,3,0:T(8,128)S(1)}, u32[]{:S(2)}) copy-start(f32[4,512,128,4]{2,1,3,0:T(8,128)S(1)} %get-tuple-element.46) | copy-start | bytes 12582916
  78.3 3.3 %copy-start.6 = (f32[128,4,4,128]{0,3,2,1:T(8,128)S(1)}, f32[128,4,4,128]{0,3,2,1:T(8,128)}, u32[]{:S(2)}) copy-start(f32[128,4,4,128]{0,3,2,1:T(8,128)} %fusion.17) | copy-start | bytes 3145732
Sparse Core Ops, SparseCore 0:
  22.7 21.2 reduce-scatter.9
  46.9 31.3 reduce-scatter.11
  80.7 19.1 reduce-scatter.13
